TPU v7x, 256 devices: a whole 4x4x8 slice. The times are simulated.
256 devices in a mesh: dp: 64 (over x, z, core), rep: 4 (over y).
Axes of the slice: x: 4, y: 4, z: 8, core: 2. Of those that a mesh axis runs over, the one named last changes fastest.
Arguments:
- frames_in: bfloat16 [4, 57344, 1536], P('rep', 'dp')
- lengths: int32 [4, 64, 4], P('rep', 'dp'), may hold values from 1 to 893, as said below
- norm_gain: float32 [1536], replicated, may hold values from 0.5 to 1.5
- norm_bias: float32 [1536], replicated, may hold values from -2 to 2
- w_in: bfloat16 [1536, 3072], P(('dp', 'rep')), may hold values from -0.15625 to 0.15625
- kernel: float32 [31, 1536], replicated, may hold values from -1 to 1
- batch_gain: float32 [1536], replicated, may hold values from 0.5 to 1.5
- batch_bias: float32 [1536], replicated, may hold values from -3 to 3
- w_out: bfloat16 [1536, 1536], P(('dp', 'rep')), may hold values from -0.15625 to 0.15625
Outputs:
- frames_out: bfloat16 [4, 57344, 1536], P('rep', 'dp')
Inputs may be any that keep to these rules, and one draw needn't show every extreme that they name: `lengths`: for each rep index, the devices 2k and 2k + 1 of dp hold 1024 frames together, so each rep index holds 512 frames for each of its dp devices; a device holds at most 896 frames, and some device of every rep index holds exactly 896.
All inputs are finite; a program needn't handle non-finite values.
Results may differ from a plain program's by a relative error of at most 0.0038.
Values may be sent and summed in bfloat16 or wider, within the bound.
A program may use at most 128 MiB of HBM per device.

v0:
```python
import jax
import jax.numpy as jnp
from jax import lax
from jax.sharding import PartitionSpec as P

FR_DEV = 512


EPSILON = 1e-05


def layer_norm(frames, norm_gain, norm_bias):
    values = frames.astype(jnp.float32)
    average = jnp.mean(values, axis=-1, keepdims=True)
    centred = values - average
    spread = jnp.mean(centred * centred, axis=-1, keepdims=True)
    return centred * lax.rsqrt(spread + EPSILON) * norm_gain + norm_bias


def depthwise(gated, labels, kernel):
    half_kernel = kernel.shape[0] // 2
    length_rows = gated.shape[0]
    padded = jnp.pad(gated, ((half_kernel, half_kernel), (0, 0)))
    padded_labels = jnp.pad(labels, (half_kernel, half_kernel), constant_values=-1)
    summed = jnp.zeros(gated.shape, jnp.float32)
    for offset in range(kernel.shape[0]):
        shared = padded_labels[offset : offset + length_rows] == labels
        contribution = jnp.where(
            shared[:, None], padded[offset : offset + length_rows].astype(jnp.float32), 0.0
        )
        summed = summed + contribution * kernel[offset]
    return summed


def project_in(normed, weight_rows):
    return jnp.dot(normed, weight_rows, preferred_element_type=jnp.float32)


def project_out(active, weight_rows):
    return jnp.dot(active, weight_rows, preferred_element_type=jnp.float32)


def on_device(
    frames_in, lengths, norm_gain, norm_bias, w_in, kernel, batch_gain, batch_bias, w_out
):
    local_frames = frames_in[0]
    local_lengths = lengths[0, 0]
    capacity = local_frames.shape[0]
    features = local_frames.shape[1]
    total_count = lax.axis_size("dp") * lax.axis_size("rep") * FR_DEV
    grouped = (w_in, w_out)
    grouped = (
        lax.all_gather(w_in, ("dp", "rep"), axis=0, tiled=True),
        lax.all_gather(w_out, ("dp", "rep"), axis=0, tiled=True),
    )
    rows_here = jnp.arange(capacity, dtype=jnp.int32)
    local_load = jnp.sum(local_lengths)
    bounds = jnp.cumsum(local_lengths)
    labels = jnp.sum((rows_here[:, None] >= bounds[None, :]).astype(jnp.int32), axis=1)
    row_weight = (rows_here < local_load).astype(jnp.float32)[:, None]
    normed = layer_norm(local_frames, norm_gain, norm_bias).astype(jnp.bfloat16)
    projected = project_in(normed, grouped[0])
    gated = (projected[:, :features] * jax.nn.sigmoid(projected[:, features:])).astype(jnp.bfloat16)
    convolved = depthwise(gated, labels, kernel)
    average = lax.psum(jnp.sum(convolved * row_weight, axis=0), ("dp", "rep")) / total_count
    centred = convolved - average
    spread = lax.psum(jnp.sum(centred * centred * row_weight, axis=0), ("dp", "rep")) / total_count
    scaled = centred * lax.rsqrt(spread + EPSILON) * batch_gain + batch_bias
    active = jax.nn.silu(scaled).astype(jnp.bfloat16)
    branch = project_out(active, grouped[1])
    mixed = (local_frames.astype(jnp.float32) + branch).astype(jnp.bfloat16)
    result = jnp.where(rows_here[:, None] < local_load, mixed, jnp.zeros_like(mixed))
    return result[None]


def solution(mesh):
    placed = (
        P("rep", "dp", None),
        P("rep", "dp", None),
        P(),
        P(),
        P(("dp", "rep"), None),
        P(),
        P(),
        P(),
        P(("dp", "rep"), None),
    )
    return jax.shard_map(
        on_device, mesh=mesh, in_specs=placed, out_specs=P("rep", "dp", None), check_vma=False
    )
```

profile of v0, /device:TPU:1, one launch (start us, length us, event | category | flops | bytes accessed | tf_op | source)
XLA Modules:
  0.0 487.7 jit_solution(4124133330554323458)
XLA Ops:
  6.5 0.0 all-gather.7.cloned.1.call-start
  6.5 0.7 all-gather.7.cloned.1.call-update
  7.3 0.0 all-gather.5.cloned.1.call-start
  7.3 0.7 all-gather.5.cloned.1.call-update
  8.0 1.3 reduce_sum.54
  9.3 0.8 reduce-window.8
  10.1 0.6 iota_compare_fusion.1
  10.8 0.7 fusion.26
  11.4 0.1 convert_reduce_fusion.1
  11.5 1.5 slice_reduce_fusion.29
  13.0 1.8 slice_reduce_fusion.30
  14.9 0.1 slice_compare_fusion.26
  14.9 2.2 convert_reduce_fusion
  17.2 2.6 fusion.4
  19.8 0.1 slice_compare_fusion.29
  19.9 0.1 slice_compare_fusion.28
  20.0 0.1 slice_compare_fusion.27
  20.1 111.2 %all-gather.7.cloned.1.call-done = bf16[256,6,1536]{2,1,0:T(8,128)(2,1)} async-done(((bf16[1,6,1536]{2,1,0:T(8,128)(2,1)}), bf16[256,6,1536]{2,1,0:T(8,128)(2,1)}) %all-gather.7.cloned.1.call-update) | async-done | bytes 4718608 | tf_op jit(solution)/shard_map/all_gather | solution.py:54
  131.3 8.5 %reshape.87 = bf16[1536,1536]{1,0:T(8,128)(2,1)} reshape(bf16[256,6,1536]{2,1,0:T(8,128)(2,1)} %all-gather.7.cloned.1.call-done) | data formatting | bytes 9437184
  139.8 0.0 copy-start
  139.8 0.0 copy-start.2
  139.8 0.0 copy-start.3
  139.8 113.5 %all-gather.5.cloned.1.call-done = bf16[256,6,3072]{2,1,0:T(8,128)(2,1)} async-done(((bf16[1,6,3072]{2,1,0:T(8,128)(2,1)}), bf16[256,6,3072]{2,1,0:T(8,128)(2,1)}) %all-gather.5.cloned.1.call-update) | async-done | bytes 9437200 | tf_op jit(solution)/shard_map/all_gather | solution.py:53
  253.3 14.2 %reshape.85 = bf16[1536,3072]{1,0:T(8,128)(2,1)} reshape(bf16[256,6,3072]{2,1,0:T(8,128)(2,1)} %all-gather.5.cloned.1.call-done) | data formatting | bytes 18874368
  267.5 0.0 copy-done
  267.5 0.0 copy-done.2
  267.5 0.0 copy-done.3
  267.5 11.3 %fusion.16 = f32[896,3072]{1,0:T(8,128)S(1)} fusion(bf16[1536,3072]{1,0:T(8,128)(2,1)} %reshape.85, bf16[1,896,1536]{2,1,0:T(8,128)(2,1)S(1)} %copy-done, f32[1536]{0:T(1024)S(1)} %copy-done.2, f32[1536]{0:T(1024)S(1)} %copy-done.3, f32[896]{0:T(1024)S(1)} %add_rsqrt_fusion.1, f32[896]{0:T(1024)S(1)} %broadcast_multiply_fusion.1), kind=kOutput, calls=%fused_computation.23 | convolution fusion | flops 8463974400 | bytes 23219200 | tf_op jit(solution)/shard_map/dot_general | solution.py:36
  278.8 1.5 fusion.13
  280.4 0.0 copy-start.4
  280.4 0.0 copy-start.5
  280.4 38.3 %multiply_reduce_fusion.1 = (f32[1536]{0:T(1024)S(1)}, f32[896,1536]{1,0:T(8,128)}) fusion(f32[896]{0:T(1024)S(1)} %fusion.26, f32[1536]{0:T(1024)S(1)} %get-tuple-element.34, pred[896]{0:T(1024)(128)(4,1)S(1)} %get-tuple-element.67, f32[1536]{0:T(1024)S(1)} %get-tuple-element.35, pred[896]{0:T(1024)(128)(4,1)S(1)} %get-tuple-element.39, ...), kind=kLoop, calls=%fused_computation.18 | loop fusion | flops 170654208 | bytes 8484608 | tf_op jit(solution)/shard_map/reduce_sum | solution.py:65
  318.7 0.0 copy-start.1
  318.7 74.8 %psum.14 = f32[1536]{0:T(1024)S(1)} all-reduce(f32[1536]{0:T(1024)S(1)} %get-tuple-element.36), channel_id=1, replica_groups=mesh['dp'=64,'rep'=4] {'dp','rep'}, use_global_device_ids=true, to_apply=%region_6.7 | all-reduce | flops 1536 | bytes 12288 | tf_op jit(solution)/shard_map/psum | solution.py:65
  393.5 3.3 multiply_reduce_fusion
  396.8 73.6 %psum.15 = f32[1536]{0:T(1024)S(1)} all-reduce(f32[1536]{0:T(1024)S(1)} %multiply_reduce_fusion), channel_id=1, replica_groups=mesh['dp'=64,'rep'=4] {'dp','rep'}, use_global_device_ids=true, to_apply=%region_8.9 | all-reduce | flops 1536 | bytes 12288 | tf_op jit(solution)/shard_map/psum | solution.py:67
  470.4 0.0 copy-done.4
  470.4 0.0 copy-done.5
  470.4 0.0 copy-done.1
  470.4 10.4 %fusion.15 = bf16[1,896,1536]{2,1,0:T(8,128)(2,1)} fusion(bf16[1536,1536]{1,0:T(8,128)(2,1)} %reshape.87, bf16[1,896,1536]{2,1,0:T(8,128)(2,1)S(1)} %copy-done.1, f32[896,1536]{1,0:T(8,128)} %get-tuple-element.37, f32[1536]{0:T(1024)S(1)} %copy-done.4, f32[1536]{0:T(1024)S(1)} %copy-done.5, f32[1536]{0:T(1024)S(1)} %add_rsqrt_fusion, ...), kind=kOutput, calls=%fused_computation.22 | convolution fusion | flops 4245749760 | bytes 15754112 | tf_op jit(solution)/shard_map/dot_general | solution.py:40
  (4 shorter events, 0.0 us)
Async XLA Ops:
  6.5 124.8 %all-gather.7.cloned.1.call-start = ((), (), s32[]{:S(2)}) async-start(), calls=%async_computation.1 | async-start | bytes 6316032 | tf_op jit(solution)/shard_map/all_gather | solution.py:54
  7.3 246.1 %all-gather.5.cloned.1.call-start = ((), (), s32[]{:S(2)}) async-start(), calls=%async_computation | async-start | bytes 12632064 | tf_op jit(solution)/shard_map/all_gather | solution.py:53
  139.8 127.7 %copy-start = (bf16[1,896,1536]{2,1,0:T(8,128)(2,1)S(1)}, bf16[1,896,1536]{2,1,0:T(8,128)(2,1)}, u32[]{:S(2)}) copy-start(bf16[1,896,1536]{2,1,0:T(8,128)(2,1)} %param.9) | copy-start | bytes 8257540
  139.8 127.7 %copy-start.2 = (f32[1536]{0:T(1024)S(1)}, f32[1536]{0:T(1024)}, u32[]{:S(2)}) copy-start(f32[1536]{0:T(1024)} %param.12) | copy-start | bytes 18436
  139.8 127.7 %copy-start.3 = (f32[1536]{0:T(1024)S(1)}, f32[1536]{0:T(1024)}, u32[]{:S(2)}) copy-start(f32[1536]{0:T(1024)} %param.11) | copy-start | bytes 18436
  280.4 190.1 %copy-start.4 = (f32[1536]{0:T(1024)S(1)}, f32[1536]{0:T(1024)}, u32[]{:S(2)}) copy-start(f32[1536]{0:T(1024)} %param.16) | copy-start | bytes 18436
  280.4 190.1 %copy-start.5 = (f32[1536]{0:T(1024)S(1)}, f32[1536]{0:T(1024)}, u32[]{:S(2)}) copy-start(f32[1536]{0:T(1024)} %param.15) | copy-start | bytes 18436
  318.7 151.7 %copy-start.1 = (bf16[1,896,1536]{2,1,0:T(8,128)(2,1)S(1)}, bf16[1,896,1536]{2,1,0:T(8,128)(2,1)}, u32[]{:S(2)}) copy-start(bf16[1,896,1536]{2,1,0:T(8,128)(2,1)} %param.9) | copy-start | bytes 8257540
Sparse Core Ops, SparseCore 0:
  11.2 120.0 all-gather.6
  135.1 118.1 all-gather.4
where the time goes:
time: 489 us; the launch traced here: 488 us
  waiting for transfers between devices  226 us (46%)
  blocking collectives  148 us (30%)
  other arithmetic  51.8 us (11%)
  local copies, waits for them, and re-layouts  26 us (5%)
  matrix products  21.8 us (4%)
  between operations  13.5 us (3%)
    all_gather x1, waiting for transfers between devices, on_device(): lax.all_gather(w_in, ('dp', 'rep'), axis=0, tiled=True)  114 us
    all_gather x1, waiting for transfers between devices, on_device(): lax.all_gather(w_out, ('dp', 'rep'), axis=0, tiled=True)  111 us
    psum x1, blocking collectives, on_device(): lax.psum(jnp.sum(convolved * row_weight, axis=0), ('dp', 'rep'))  74.8 us
    psum x1, blocking collectives, on_device(): lax.psum(jnp.sum(centred * centred * row_weight, axis=0), ('dp', 'rep'))  73.6 us
    reduce_sum x1, other arithmetic, on_device(): jnp.sum(convolved * row_weight, axis=0)  38.3 us
    unnamed x14, local copies, waits for them, and re-layouts  22.6 us
    dot_general x1, matrix products, project_in(): return jnp.dot(normed, weight_rows, preferred_element_type=jnp.float32)  11.3 us
    dot_general x1, matrix products, project_out(): return jnp.dot(active, weight_rows, preferred_element_type=jnp.float32)  10.4 us
  transfers between devices with their start and end apart: 2, of which 2 were waited for; matrix products, arithmetic and copies ran while one was open for 4% of the time, Pallas kernels for 0%

commit v1 on v0

v1 whole, which is shorter than its diff:
```python
import functools

import jax
import jax.numpy as jnp
import numpy as np
from jax import lax
from jax.experimental import pallas as pl
from jax.experimental.pallas import tpu as pltpu
from jax.sharding import PartitionSpec as P

EPSILON = 1e-05
MESH = pl.DeviceIdType.MESH
F32 = jnp.float32
BF16 = jnp.bfloat16

NX, NY, NZ, NC = 4, 4, 8, 2
D = 1536
HALF = D // 2
CAP = 896
PAIR = 1024
GAP = 15
ROWS = 1152
BLK = 128
NB = ROWS // BLK
WIN = 192
TAPS = 31
N_IN = 6
N_OUT = 3
NCH = N_IN + N_OUT
TOTAL = 512 * 256


def feature_order():
    order = np.zeros((384, 384), np.float32)
    for z in range(8):
        for c in range(2):
            for y in range(4):
                for i in range(6):
                    order[z * 48 + c * 24 + y * 6 + i, y * 96 + z * 12 + c * 6 + i] = 1.0
    return order


def compaction():
    pick = np.zeros((96, 128), np.float32)
    for k in range(16):
        for i in range(6):
            pick[k * 6 + i, k * 8 + i] = 1.0
    return pick


def kernel(
    lengths_ref, x_ref, gain_ref, bias_ref, w_in_ref, w_out_ref, taps_ref, bgain_ref, bbias_ref,
    order_ref, pick_ref,
    out_ref,
    slab, zin, weights, xs, normed_own, normed_mate, mask_own, mask_mate,
    proj, gated, conv, act, w_nat, st_own, st_a, st_b0, st_b, stats,
    z_send, z_recv, ring_send, r1_recv, r2_recv, n_send, n_recv, m_send, m_recv,
    c_send, c_recv, w_send, w_recv, sa_send, sa_recv, sb_send, sb_recv,
):
    dp = lax.axis_index("dp")
    y = lax.axis_index("rep")
    x = dp // 16
    z = lax.rem(dp // 2, 8)
    c = lax.rem(dp, 2)
    mate = (x * 16 + z * 2 + (1 - c), y)

    def device(xx, yy, zz, cc):
        return (lax.rem(xx + 4, 4) * 16 + lax.rem(zz + 8, 8) * 2 + cc, lax.rem(yy + 4, 4))

    def z_peer(k):
        me = z * 2 + c
        other = lax.rem(me + k, 16)
        return other // 2, lax.rem(other, 2)

    def xy_peer(k):
        me = x * 4 + y
        other = lax.rem(me + k, 16)
        return other // 4, lax.rem(other, 4)

    barrier = pltpu.get_barrier_semaphore()

    def greet(k, carry):
        zz, cc = z_peer(k)
        pl.semaphore_signal(barrier, 1, device_id=device(x, y, zz, cc), device_id_type=MESH)
        xx, yy = xy_peer(k)
        pl.semaphore_signal(barrier, 1, device_id=device(xx, yy, z, c), device_id_type=MESH)
        return carry

    lax.fori_loop(1, 16, greet, 0)

    slab[...] = jnp.zeros_like(slab)
    for h in range(2):
        for j in range(N_IN):
            lo = h * HALF + j * 128
            slab[h, j, 0:6, 0:128] = w_in_ref[:, lo : lo + 128]
            slab[h, j, 0:6, 128:256] = w_in_ref[:, D + lo : D + lo + 128]
        for j in range(N_OUT):
            lo = h * HALF + j * 256
            slab[h, N_IN + j, 0:6, :] = w_out_ref[:, lo : lo + 256]
    for j in range(NCH):
        zin[j, z * 2 + c] = slab[c, j]

    pl.semaphore_wait(barrier, 30)

    def z_start(j):
        def one(k, carry):
            zz, cc = z_peer(k)
            pltpu.make_async_remote_copy(
                src_ref=slab.at[cc, j], dst_ref=zin.at[j, z * 2 + c],
                send_sem=z_send, recv_sem=z_recv.at[j],
                device_id=device(x, y, zz, cc), device_id_type=MESH,
            ).start()
            return carry
        lax.fori_loop(1, 16, one, 0)

    def wait_for(ref, sem):
        pltpu.make_async_copy(ref, ref, sem).wait()

    def first_axis(j):
        f = lax.rem(c + j, 2)
        d = 1 - 2 * lax.rem(j // 2, 2)
        return f, d

    def along(f, step):
        return x + (1 - f) * step, y + f * step

    def ring1_copy(j, f, origin, to, slot):
        ox, oy = along(f, origin)
        tx, ty = along(f, to)
        ref = weights.at[j * 16 + lax.rem(ox + 4, 4) * 4 + lax.rem(oy + 4, 4)]
        pltpu.make_async_remote_copy(
            src_ref=ref, dst_ref=ref, send_sem=ring_send, recv_sem=r1_recv.at[j, slot],
            device_id=device(tx, ty, z, c), device_id_type=MESH,
        ).start()

    def ring2_copy(j, f, origin, to, slot):
        s = 1 - f
        ox, oy = along(s, origin)
        tx, ty = along(s, to)
        ox, oy = lax.rem(ox + 4, 4), lax.rem(oy + 4, 4)
        for k in range(4):
            ref = weights.at[j * 16 + jnp.where(f == 0, k * 4 + oy, ox * 4 + k)]
            pltpu.make_async_remote_copy(
                src_ref=ref, dst_ref=ref, send_sem=ring_send, recv_sem=r2_recv.at[j, slot],
                device_id=device(tx, ty, z, c), device_id_type=MESH,
            ).start()

    def e1(j):
        wait_for(zin.at[0, pl.ds(0, 15)], z_recv.at[j])
        rows = zin[j].reshape(128, 256)
        block = jnp.dot(pick_ref[...], rows, preferred_element_type=F32).astype(BF16)
        weights[j * 16 + x * 4 + y] = block
        f, _ = first_axis(j)
        ring1_copy(j, f, 0, 1, 0)
        ring1_copy(j, f, 0, -1, 1)

    def e2(j):
        f, d = first_axis(j)
        wait_for(weights.at[0], r1_recv.at[j, 0])
        wait_for(weights.at[0], r1_recv.at[j, 1])
        ring1_copy(j, f, -d, d, 2)

    def e3(j):
        f, _ = first_axis(j)
        wait_for(weights.at[0], r1_recv.at[j, 2])
        ring2_copy(j, f, 0, 1, 0)
        ring2_copy(j, f, 0, -1, 1)

    def e4(j):
        f, d = first_axis(j)
        wait_for(weights.at[pl.ds(0, 4)], r2_recv.at[j, 0])
        wait_for(weights.at[pl.ds(0, 4)], r2_recv.at[j, 1])
        ring2_copy(j, f, -d, d, 2)

    def e5(j):
        wait_for(weights.at[pl.ds(0, 4)], r2_recv.at[j, 2])

    n_own = lengths_ref[0] + lengths_ref[1] + lengths_ref[2] + lengths_ref[3]
    b0 = lengths_ref[0]
    b1 = b0 + lengths_ref[1]
    b2 = b1 + lengths_ref[2]
    base = c * (PAIR - n_own + 4 * GAP)

    def place(i):
        u = (i >= b0).astype(jnp.int32) + (i >= b1).astype(jnp.int32) + (i >= b2).astype(jnp.int32)
        return i + base + GAP * u

    def window(ref, w):
        return jnp.concatenate([ref[w + k] for k in range(WIN // 16)], axis=0)

    def layer_norm_block(qi):
        q = qi + c
        low = jnp.maximum(q * BLK - base - 3 * GAP, 0)
        w = jnp.minimum(lax.div(low, 16), (CAP - WIN) // 16)
        i = w * 16 + lax.broadcasted_iota(jnp.int32, (BLK, WIN), 1)
        r = q * BLK + lax.broadcasted_iota(jnp.int32, (BLK, WIN), 0)
        chosen = jnp.logical_and(place(i) == r, i < n_own).astype(F32)
        xs[...] = jnp.dot(chosen.astype(BF16), window(x_ref, w), preferred_element_type=F32)
        live = jnp.broadcast_to(jnp.sum(chosen, axis=1, keepdims=True), (BLK, 128))
        mask_own[q] = live

        def rows(g, carry):
            at = pl.ds(pl.multiple_of(g * 16, 16), 16)
            v = xs[at, :]
            average = jnp.sum(v, axis=1, keepdims=True) * (1.0 / D)
            centred = v - average
            spread = jnp.sum(centred * centred, axis=1, keepdims=True) * (1.0 / D)
            res = centred * lax.rsqrt(spread + EPSILON) * gain_ref[...] + bias_ref[...]
            m = mask_own[q, at, 0:1]
            normed_own[q, at, :] = jnp.where(m > 0.0, res, 0.0).astype(BF16)
            return carry

        lax.fori_loop(0, BLK // 16, rows, 0)
        for g in range(4):
            cols = slice(g * 384, (g + 1) * 384)
            normed_own[q, :, cols] = jnp.dot(
                normed_own[q, :, cols], order_ref[...], preferred_element_type=F32
            ).astype(BF16)
        pltpu.make_async_remote_copy(
            src_ref=normed_own.at[q], dst_ref=normed_mate.at[q], send_sem=n_send, recv_sem=n_recv,
            device_id=mate, device_id_type=MESH,
        ).start()

    def project(j):
        w = weights[pl.ds(j * 16, 16)].reshape(D, 256)

        def rows(b, carry):
            at = pl.ds(b * 3, 3)
            proj[...] = jnp.dot(
                normed_own[at].reshape(3 * BLK, D), w, preferred_element_type=F32
            )
            v = proj[:, 0:128]
            g = proj[:, 128:256]
            res = v * jax.nn.sigmoid(g)
            gated[pl.ds(pl.multiple_of(16 + b * 3 * BLK, 16), 3 * BLK), :] = res.astype(BF16).astype(F32)
            return carry

        lax.fori_loop(0, NB // 3, rows, 0)

    def convolve(j):
        cc = c * N_IN + j
        lanes = pl.ds(pl.multiple_of(cc * 128, 128), 128)
        taps = taps_ref[:, lanes]

        def rows(b, total):
            r0 = pl.multiple_of(b * BLK, BLK)
            v = gated[pl.ds(r0, BLK + 32), :]
            acc = jnp.zeros((BLK, 128), F32)
            for r in range(8):
                turned = v if r == 0 else pltpu.roll(v, BLK + 32 - r, axis=0)
                for m in range(4):
                    o = 8 * m + r - 1
                    if 0 <= o < TAPS:
                        acc = acc + turned[8 * m : 8 * m + BLK] * taps[o : o + 1]
            acc = acc * mask_own[b]
            conv[cc, pl.ds(r0, BLK), :] = acc
            return total + jnp.sum(acc.reshape(BLK // 8, 8, 128), axis=0)

        total = lax.fori_loop(0, NB, rows, jnp.zeros((8, 128), F32))
        average = jnp.sum(total, axis=0, keepdims=True) * (1.0 / PAIR)

        def deviations(b, total):
            r0 = pl.multiple_of(b * BLK, BLK)
            diff = (conv[cc, pl.ds(r0, BLK), :] - average) * mask_own[b]
            return total + jnp.sum((diff * diff).reshape(BLK // 8, 8, 128), axis=0)

        square = lax.fori_loop(0, NB, deviations, jnp.zeros((8, 128), F32))
        st_own[0, j] = average
        st_own[1, j] = jnp.sum(square, axis=0, keepdims=True)
        at = pl.ds(pl.multiple_of((1 - c) * BLK, BLK), PAIR)
        pltpu.make_async_remote_copy(
            src_ref=conv.at[cc, at], dst_ref=conv.at[cc, at], send_sem=c_send, recv_sem=c_recv,
            device_id=mate, device_id_type=MESH,
        ).start()

    def natural(j):
        for g in range(4):
            part = weights[pl.ds((N_IN + j) * 16 + g * 4, 4)].reshape(384, 256)
            w_nat[c, j, g * 384 : (g + 1) * 384, :] = jnp.dot(
                order_ref[...], part, preferred_element_type=F32
            ).astype(BF16)
        pltpu.make_async_remote_copy(
            src_ref=w_nat.at[c, j], dst_ref=w_nat.at[c, j], send_sem=w_send, recv_sem=w_recv,
            device_id=mate, device_id_type=MESH,
        ).start()

    def loop(lo, hi, f):
        lax.fori_loop(lo, hi, lambda k, carry: (f(k), carry)[1], 0)

    gated[0:16, :] = jnp.zeros((16, 128), F32)
    gated[ROWS + 16 : ROWS + 32, :] = jnp.zeros((16, 128), F32)

    loop(0, NCH, z_start)
    normed_own[8 * (1 - c)] = jnp.zeros((BLK, D), BF16)
    mask_own[8 * (1 - c)] = jnp.zeros((BLK, 128), F32)

    e1(0)
    loop(0, 2, layer_norm_block)
    e2(0)
    loop(2, 4, layer_norm_block)
    e1(1)
    e3(0)
    loop(4, 6, layer_norm_block)
    e2(1)
    e4(0)
    loop(6, 8, layer_norm_block)
    masks = pl.ds(c, 8)
    pltpu.make_async_remote_copy(
        src_ref=mask_own.at[masks], dst_ref=mask_mate.at[masks], send_sem=m_send, recv_sem=m_recv,
        device_id=mate, device_id_type=MESH,
    ).start()
    normed_mate[8 * c] = jnp.zeros((BLK, D), BF16)
    mask_mate[8 * c] = jnp.zeros((BLK, 128), F32)
    wait_for(normed_mate.at[pl.ds(0, 8)], n_send)
    wait_for(mask_mate.at[pl.ds(0, 8)], m_send)
    wait_for(normed_mate.at[pl.ds(0, 8)], n_recv)
    wait_for(mask_mate.at[pl.ds(0, 8)], m_recv)

    def join(q):
        normed_own[q] = normed_own[q] + normed_mate[q]
        mask_own[q] = mask_own[q] + mask_mate[q]

    loop(0, NB, join)

    def slot(m):
        pl.when(m < NCH)(lambda: e1(m))
        pl.when(m < NCH + 1)(lambda: e3(m - 1))
        e5(m - 2)
        pl.when(m - 2 < N_IN)(lambda: project(m - 2))
        pl.when(m - 2 >= N_IN)(lambda: natural(m - 2 - N_IN))
        pl.when(m < NCH)(lambda: e2(m))
        pl.when(m < NCH + 1)(lambda: e4(m - 1))
        pl.when(m - 2 < N_IN)(lambda: convolve(m - 2))

    loop(2, N_IN + 2, slot)

    me_a = x * 4 + y
    st_a[me_a] = st_own[...]

    def send_a(k):
        xx, yy = xy_peer(k)
        pltpu.make_async_remote_copy(
            src_ref=st_own, dst_ref=st_a.at[me_a], send_sem=sa_send, recv_sem=sa_recv,
            device_id=device(xx, yy, z, c), device_id_type=MESH,
        ).start()

    loop(1, 16, send_a)
    slot(N_IN + 2)
    wait_for(st_a.at[pl.ds(0, 15)], sa_recv)
    all_a = st_a[...]
    mean_a = jnp.sum(all_a[:, 0], axis=0) * (1.0 / 16)
    off_a = all_a[:, 0] - mean_a[None]
    st_b0[0] = mean_a
    st_b0[1] = jnp.sum(all_a[:, 1], axis=0) + PAIR * jnp.sum(off_a * off_a, axis=0)
    me_b = c * 8 + z
    st_b[me_b] = st_b0[...]

    def send_b(k):
        zz, cc = z_peer(k)
        pltpu.make_async_remote_copy(
            src_ref=st_b0, dst_ref=st_b.at[me_b], send_sem=sb_send, recv_sem=sb_recv,
            device_id=device(x, y, zz, cc), device_id_type=MESH,
        ).start()

    loop(1, 16, send_b)
    slot(N_IN + 3)
    slot(N_IN + 4)
    wait_for(st_b.at[pl.ds(0, 15)], sb_recv)
    for h in range(2):
        part = st_b[h * 8 : h * 8 + 8]
        mean_b = jnp.sum(part[:, 0], axis=0) * (1.0 / 8)
        off_b = part[:, 0] - mean_b[None]
        spread = (
            jnp.sum(part[:, 1], axis=0) + (16 * PAIR) * jnp.sum(off_b * off_b, axis=0)
        ) * (1.0 / TOTAL)
        stats[0, h * 6 : h * 6 + 6] = mean_b
        stats[1, h * 6 : h * 6 + 6] = lax.rsqrt(spread + EPSILON)

    at_mine = pl.ds(pl.multiple_of(c * BLK, BLK), PAIR)
    wait_for(conv.at[pl.ds(0, 6), pl.ds(0, PAIR)], c_recv)
    wait_for(w_nat.at[0], w_recv)

    def activate(qi):
        q = qi + c
        at = pl.ds(pl.multiple_of(q * BLK, BLK), BLK)
        for cc in range(12):
            lanes = slice(cc * 128, cc * 128 + 128)
            v = conv[cc, at, :] - stats[0, cc]
            v = v * (stats[1, cc] * bgain_ref[:, lanes]) + bbias_ref[:, lanes]
            act[pl.ds(q * 8, 8), :, lanes] = jax.nn.silu(v).astype(BF16).reshape(8, 16, 128)

    loop(0, 8, activate)

    def finish(t):
        i0 = t * BLK
        low = base + i0
        w = jnp.minimum(lax.div(low, 16), (ROWS - WIN) // 16)
        i = i0 + lax.broadcasted_iota(jnp.int32, (BLK, WIN), 0)
        r = w * 16 + lax.broadcasted_iota(jnp.int32, (BLK, WIN), 1)
        chosen = jnp.logical_and(place(i) == r, i < n_own).astype(F32).astype(BF16)
        mine = jnp.dot(chosen, window(act, w), preferred_element_type=F32).astype(BF16)
        rows = pl.ds(t * 8, 8)
        live = i0 + lax.broadcasted_iota(jnp.int32, (BLK, 256), 0) < n_own
        for h in range(2):
            for k in range(N_OUT):
                lo = h * HALF + k * 256
                branch = jnp.dot(mine, w_nat[h, k], preferred_element_type=F32)
                res = x_ref[rows, :, lo : lo + 256].reshape(BLK, 256).astype(F32) + branch
                out_ref[rows, :, lo : lo + 256] = jnp.where(live, res, 0.0).astype(BF16).reshape(8, 16, 256)

    loop(0, CAP // BLK, finish)

    wait_for(zin.at[:, pl.ds(0, 15)], z_send)
    wait_for(weights.at[pl.ds(0, 135)], ring_send)
    wait_for(conv.at[pl.ds(0, 6), pl.ds(0, PAIR)], c_send)
    wait_for(w_nat.at[0], w_send)
    wait_for(st_a.at[pl.ds(0, 15)], sa_send)
    wait_for(st_b.at[pl.ds(0, 15)], sb_send)


def on_device(
    frames_in, lengths, norm_gain, norm_bias, w_in, taps, batch_gain, batch_bias, w_out
):
    vmem = pl.BlockSpec(memory_space=pltpu.VMEM)
    dma = pltpu.SemaphoreType.DMA
    out = pl.pallas_call(
        kernel,
        out_shape=jax.ShapeDtypeStruct((CAP // 16, 16, D), BF16),
        in_specs=[pl.BlockSpec(memory_space=pltpu.SMEM)] + [vmem] * 10,
        out_specs=vmem,
        scratch_shapes=[
            pltpu.VMEM((2, NCH, 8, 256), BF16),
            pltpu.VMEM((NCH, 16, 8, 256), BF16),
            pltpu.VMEM((NCH * 16, 96, 256), BF16),
            pltpu.VMEM((BLK, D), F32),
            pltpu.VMEM((NB, BLK, D), BF16),
            pltpu.VMEM((NB, BLK, D), BF16),
            pltpu.VMEM((NB, BLK, 128), F32),
            pltpu.VMEM((NB, BLK, 128), F32),
            pltpu.VMEM((3 * BLK, 256), F32),
            pltpu.VMEM((ROWS + 32, 128), F32),
            pltpu.VMEM((12, ROWS, 128), F32),
            pltpu.VMEM((ROWS // 16, 16, D), BF16),
            pltpu.VMEM((2, N_OUT, D, 256), BF16),
            pltpu.VMEM((2, 6, 1, 128), F32),
            pltpu.VMEM((16, 2, 6, 1, 128), F32),
            pltpu.VMEM((2, 6, 1, 128), F32),
            pltpu.VMEM((16, 2, 6, 1, 128), F32),
            pltpu.VMEM((2, 12, 1, 128), F32),
            dma, dma((NCH,)), dma, dma((NCH, 3)), dma((NCH, 3)),
            dma, dma, dma, dma, dma, dma, dma, dma, dma, dma, dma, dma,
        ],
        compiler_params=pltpu.CompilerParams(
            collective_id=0, has_side_effects=True, vmem_limit_bytes=60 * 2**20
        ),
        cost_estimate=pl.CostEstimate(
            flops=20 * 10**9, bytes_accessed=10**7, transcendentals=4 * 10**6
        ),
    )(
        lengths.reshape(4), frames_in.reshape(CAP // 16, 16, D), norm_gain.reshape(1, D), norm_bias.reshape(1, D),
        w_in, w_out, taps, batch_gain.reshape(1, D), batch_bias.reshape(1, D),
        jnp.asarray(feature_order(), BF16), jnp.asarray(compaction(), BF16),
    )
    return out.reshape(1, CAP, D)


def solution(mesh):
    placed = (
        P("rep", "dp", None), P("rep", "dp", None), P(), P(), P(("dp", "rep"), None),
        P(), P(), P(), P(("dp", "rep"), None),
    )
    return jax.shard_map(
        on_device, mesh=mesh, in_specs=placed, out_specs=P("rep", "dp", None), check_vma=False
    )
```

time: 489 us -> 133 us (0.27)
  waiting for transfers between devices: 226 us -> 0 us
  blocking collectives: 148 us -> 0 us
  Pallas kernels: 0 us -> 124 us
  other arithmetic: 51.8 us -> 0 us
  matrix products: 21.8 us -> 0 us
  local copies, waits for them, and re-layouts: 26 us -> 8.67 us
  between operations: 13.5 us -> 0.01 us
    all_gather x2 -> x0, waiting for transfers between devices: 225 us -> none  [the longest x1 114 us: on_device(): lax.all_gather(w_in, ('dp', 'rep'), axis=0, tiled=True)]
    psum x2 -> x0, blocking collectives: 148 us -> none  [the longest x1 74.8 us: on_device(): lax.psum(jnp.sum(convolved * row_weight, axis=0), ('dp', 'rep'))]
    pallas_call x0 -> x1, Pallas kernels: none -> 124 us  [on_device(): pl.pallas_call(kernel, out_shape=jax.ShapeDtypeStruct((CAP // 16, 16, D),...]
    reduce_sum x6 -> x0, other arithmetic: 47.9 us -> none  [the longest x1 38.3 us: on_device(): jnp.sum(convolved * row_weight, axis=0)]
    dot_general x2 -> x0, matrix products: 21.8 us -> none  [the longest x1 11.3 us: project_in(): return jnp.dot(normed, weight_rows, preferred_element_type=jnp.float32)]
    unnamed x14 -> x1, local copies, waits for them, and re-layouts: 22.6 us -> 3.49 us
    reshape x0 -> x4, local copies, waits for them, and re-layouts: none -> 5.18 us  [the longest x1 1.3 us: on_device(): batch_bias.reshape(1, D)]
  transfers between devices with their start and end apart: 2 -> 0, of which waited for: 2 -> 0; matrix products, arithmetic and copies ran while one was open for 4% -> 0% of each run, Pallas kernels for 0% -> 0%
where the time goes in v1:
time: 133 us; the launch traced here: 132 us
  Pallas kernels  124 us (93%)
  local copies, waits for them, and re-layouts  8.67 us (7%)
    pallas_call x1, Pallas kernels, on_device(): pl.pallas_call(kernel, out_shape=jax.ShapeDtypeStruct((CAP // 16, 16, D),...  124 us
    unnamed x1, local copies, waits for them, and re-layouts  3.49 us

profile of v1, /device:TPU:1, one launch (start us, length us, event | category | flops | bytes accessed | tf_op | source)
XLA Modules:
  0.0 132.3 jit_solution(13769102489326888832)
XLA Ops:
  0.0 1.3 reshape.23.gain_ref
  1.3 1.3 reshape.24.bias_ref
  2.6 1.3 reshape.25.bgain_ref
  3.9 1.3 reshape.26.bbias_ref
  5.2 123.7 %shard_map.109 = bf16[56,16,1536]{2,1,0:T(8,128)(2,1)} custom-call(s32[4]{0:T(128)} %bitcast.5, bf16[56,16,1536]{2,1,0:T(8,128)(2,1)} %bitcast.4, f32[1,1536]{1,0:T(1,128)} %reshape.23.gain_ref, f32[1,1536]{1,0:T(1,128)} %reshape.24.bias_ref, bf16[6,3072]{1,0:T(8,128)(2,1)} %w_in_ref.1, bf16[6,1536]{1,0:T(8,128)(2,1)} %w_out_ref.1, f32[31,1536]{1,0:T(8,128)} %taps_ref.1, ...), custom_call_target="tpu_custom_call" | custom-call | flops 20000000000 | bytes 10000000 | tf_op jit(solution)/shard_map/pallas_call | solution.py:426
  128.9 3.5 %copy.13 = bf16[1,896,1536]{2,1,0:T(8,128)(2,1)} copy(bf16[1,896,1536]{2,1,0:T(8,128)(2,1)} %bitcast.3) | data formatting | bytes 5505024

commit v2 on v1

--- a/solution.py
+++ b/solution.py
@@ -25,8 +25,6 @@
 WIN = 192
 TAPS = 31
 N_IN = 6
-N_OUT = 3
-NCH = N_IN + N_OUT
 TOTAL = 512 * 256
 
 
@@ -52,9 +50,9 @@
     lengths_ref, x_ref, gain_ref, bias_ref, w_in_ref, w_out_ref, taps_ref, bgain_ref, bbias_ref,
     order_ref, pick_ref,
     out_ref,
-    slab, zin, weights, xs, normed_own, normed_mate, mask_own, mask_mate,
+    slab, slab_o, zin, zin_o, weights, wout, xs, normed_own, normed_mate, mask_own, mask_mate,
     proj, gated, conv, act, w_nat, st_own, st_a, st_b0, st_b, stats,
-    z_send, z_recv, ring_send, r1_recv, r2_recv, n_send, n_recv, m_send, m_recv,
+    z_send, zo_send, z_recv, r1_send, r2_send, r3_send, r1_recv, r2_recv, r3_recv, n_send, n_recv, m_send, m_recv,
     c_send, c_recv, w_send, w_recv, sa_send, sa_recv, sb_send, sb_recv,
 ):
     dp = lax.axis_index("dp")
@@ -62,118 +60,123 @@
     x = dp // 16
     z = lax.rem(dp // 2, 8)
     c = lax.rem(dp, 2)
-    mate = (x * 16 + z * 2 + (1 - c), y)
-
-    def device(xx, yy, zz, cc):
-        return (lax.rem(xx + 4, 4) * 16 + lax.rem(zz + 8, 8) * 2 + cc, lax.rem(yy + 4, 4))
-
-    def z_peer(k):
-        me = z * 2 + c
-        other = lax.rem(me + k, 16)
-        return other // 2, lax.rem(other, 2)
-
-    def xy_peer(k):
-        me = x * 4 + y
-        other = lax.rem(me + k, 16)
-        return other // 4, lax.rem(other, 4)
+    flips = [(1 - 2 * lax.rem(dp // 2**b, 2)) * 2**b for b in range(6)]
+    y_flips = [(1 - 2 * lax.rem(y // 2**b, 2)) * 2**b for b in range(2)]
+
+    def flip(start, deltas, k):
+        for b, delta in enumerate(deltas):
+            if k >> b & 1:
+                start = start + delta
+        return start
+
+    mate = (flip(dp, flips, 1), y)
+    z_peers = [(flip(dp, flips, k), y) for k in range(16)]
+    xy_peers = [(flip(dp, flips, (k >> 2) << 4), flip(y, y_flips, k & 3)) for k in range(16)]
+    xs_at = [lax.rem(x + k, 4) for k in range(4)]
+    ys_at = [lax.rem(y + k, 4) for k in range(4)]
+    me_z = z * 2 + c
+    me_xy = x * 4 + y
 
     barrier = pltpu.get_barrier_semaphore()
-
-    def greet(k, carry):
-        zz, cc = z_peer(k)
-        pl.semaphore_signal(barrier, 1, device_id=device(x, y, zz, cc), device_id_type=MESH)
-        xx, yy = xy_peer(k)
-        pl.semaphore_signal(barrier, 1, device_id=device(xx, yy, z, c), device_id_type=MESH)
-        return carry
-
-    lax.fori_loop(1, 16, greet, 0)
+    for k in range(1, 16):
+        pl.semaphore_signal(barrier, 1, device_id=z_peers[k], device_id_type=MESH)
+        pl.semaphore_signal(barrier, 1, device_id=xy_peers[k], device_id_type=MESH)
 
     slab[...] = jnp.zeros_like(slab)
+    slab_o[...] = jnp.zeros_like(slab_o)
     for h in range(2):
         for j in range(N_IN):
             lo = h * HALF + j * 128
-            slab[h, j, 0:6, 0:128] = w_in_ref[:, lo : lo + 128]
-            slab[h, j, 0:6, 128:256] = w_in_ref[:, D + lo : D + lo + 128]
-        for j in range(N_OUT):
-            lo = h * HALF + j * 256
-            slab[h, N_IN + j, 0:6, :] = w_out_ref[:, lo : lo + 256]
-    for j in range(NCH):
-        zin[j, z * 2 + c] = slab[c, j]
+            slab[h, j // 2, j % 2, 0:6, 0:128] = w_in_ref[:, lo : lo + 128]
+            slab[h, j // 2, j % 2, 0:6, 128:256] = w_in_ref[:, D + lo : D + lo + 128]
+        for j in range(2):
+            lo = h * HALF + j * 384
+            slab_o[h, j, 0:6, :] = w_out_ref[:, lo : lo + 384]
+    for p in range(3):
+        zin[p, me_z] = slab[c, p]
+    zin_o[me_z] = slab_o[c]
 
     pl.semaphore_wait(barrier, 30)
 
-    def z_start(j):
-        def one(k, carry):
-            zz, cc = z_peer(k)
-            pltpu.make_async_remote_copy(
-                src_ref=slab.at[cc, j], dst_ref=zin.at[j, z * 2 + c],
-                send_sem=z_send, recv_sem=z_recv.at[j],
-                device_id=device(x, y, zz, cc), device_id_type=MESH,
-            ).start()
-            return carry
-        lax.fori_loop(1, 16, one, 0)
+    def send(src, dst, sent, landed, to):
+        pltpu.make_async_remote_copy(
+            src_ref=src, dst_ref=dst, send_sem=sent, recv_sem=landed,
+            device_id=to, device_id_type=MESH,
+        ).start()
 
     def wait_for(ref, sem):
         pltpu.make_async_copy(ref, ref, sem).wait()
 
-    def first_axis(j):
-        f = lax.rem(c + j, 2)
-        d = 1 - 2 * lax.rem(j // 2, 2)
-        return f, d
-
-    def along(f, step):
-        return x + (1 - f) * step, y + f * step
-
-    def ring1_copy(j, f, origin, to, slot):
-        ox, oy = along(f, origin)
-        tx, ty = along(f, to)
-        ref = weights.at[j * 16 + lax.rem(ox + 4, 4) * 4 + lax.rem(oy + 4, 4)]
-        pltpu.make_async_remote_copy(
-            src_ref=ref, dst_ref=ref, send_sem=ring_send, recv_sem=r1_recv.at[j, slot],
-            device_id=device(tx, ty, z, c), device_id_type=MESH,
-        ).start()
-
-    def ring2_copy(j, f, origin, to, slot):
-        s = 1 - f
-        ox, oy = along(s, origin)
-        tx, ty = along(s, to)
-        ox, oy = lax.rem(ox + 4, 4), lax.rem(oy + 4, 4)
-        for k in range(4):
-            ref = weights.at[j * 16 + jnp.where(f == 0, k * 4 + oy, ox * 4 + k)]
-            pltpu.make_async_remote_copy(
-                src_ref=ref, dst_ref=ref, send_sem=ring_send, recv_sem=r2_recv.at[j, slot],
-                device_id=device(tx, ty, z, c), device_id_type=MESH,
-            ).start()
-
-    def e1(j):
-        wait_for(zin.at[0, pl.ds(0, 15)], z_recv.at[j])
-        rows = zin[j].reshape(128, 256)
-        block = jnp.dot(pick_ref[...], rows, preferred_element_type=F32).astype(BF16)
-        weights[j * 16 + x * 4 + y] = block
-        f, _ = first_axis(j)
-        ring1_copy(j, f, 0, 1, 0)
-        ring1_copy(j, f, 0, -1, 1)
-
-    def e2(j):
-        f, d = first_axis(j)
-        wait_for(weights.at[0], r1_recv.at[j, 0])
-        wait_for(weights.at[0], r1_recv.at[j, 1])
-        ring1_copy(j, f, -d, d, 2)
-
-    def e3(j):
-        f, _ = first_axis(j)
-        wait_for(weights.at[0], r1_recv.at[j, 2])
-        ring2_copy(j, f, 0, 1, 0)
-        ring2_copy(j, f, 0, -1, 1)
-
-    def e4(j):
-        f, d = first_axis(j)
-        wait_for(weights.at[pl.ds(0, 4)], r2_recv.at[j, 0])
-        wait_for(weights.at[pl.ds(0, 4)], r2_recv.at[j, 1])
-        ring2_copy(j, f, -d, d, 2)
-
-    def e5(j):
-        wait_for(weights.at[pl.ds(0, 4)], r2_recv.at[j, 2])
+    def s0(p):
+        for k in range(1, 16):
+            other = 1 - c if k % 2 else c
+            if p < 3:
+                send(slab.at[other, p], zin.at[p, me_z], z_send, z_recv.at[p], z_peers[k])
+            else:
+                send(slab_o.at[other], zin_o.at[me_z], zo_send, z_recv.at[p], z_peers[k])
+
+    def chunk(p, a):
+        return weights.at[2 * p + a] if p < 3 else wout.at[a]
+
+    def kind(p):
+        return 0 if p < 3 else 1
+
+    def for_core(f):
+        pl.when(c == 0)(lambda: f(0))
+        pl.when(c == 1)(lambda: f(1))
+
+    def s1(p):
+        if p < 3:
+            wait_for(zin.at[0, pl.ds(0, 15)], z_recv.at[p])
+        else:
+            wait_for(zin_o.at[pl.ds(0, 15)], z_recv.at[p])
+        for a in range(2):
+            rows = (zin[p, :, a] if p < 3 else zin_o[:, a]).reshape(128, 256 if p < 3 else 384)
+            chunk(p, a)[x, y] = jnp.dot(
+                pick_ref[...], rows, preferred_element_type=F32
+            ).astype(BF16)
+
+        def go(v):
+            for a in range(2):
+                ref = chunk(p, a).at[x, y]
+                for k in (1, 3, 2):
+                    to = (dp + (xs_at[k] - x) * 16, y) if (v + a) % 2 == 0 else (dp, ys_at[k])
+                    send(ref, ref, r1_send.at[kind(p)], r1_recv.at[p], to)
+
+        for_core(go)
+
+    def second(p, a, v, origin, part):
+        if (v + a) % 2 == 0:
+            return chunk(p, a).at[part, ys_at[origin]]
+        return chunk(p, a).at[xs_at[origin], part]
+
+    def second_to(a, v, k):
+        return (dp, ys_at[k]) if (v + a) % 2 == 0 else (dp + (xs_at[k] - x) * 16, y)
+
+    def s2(p):
+        wait_for(chunk(p, 0).at[pl.ds(0, 2), pl.ds(0, 3)], r1_recv.at[p])
+
+        def go(v):
+            for a in range(2):
+                ref = second(p, a, v, 0, pl.ds(0, 4))
+                for k in (1, 3):
+                    send(ref, ref, r2_send.at[kind(p)], r2_recv.at[p], second_to(a, v, k))
+
+        for_core(go)
+
+    def s3(p):
+        wait_for(chunk(p, 0), r2_recv.at[p])
+
+        def go(v):
+            for a in range(2):
+                for k, part in ((1, pl.ds(0, 2)), (3, pl.ds(2, 2))):
+                    ref = second(p, a, v, 4 - k, part)
+                    send(ref, ref, r3_send.at[kind(p)], r3_recv.at[p], second_to(a, v, k))
+
+        for_core(go)
+
+    def s4(p):
+        wait_for(chunk(p, 0).at[pl.ds(0, 2)], r3_recv.at[p])
 
     n_own = lengths_ref[0] + lengths_ref[1] + lengths_ref[2] + lengths_ref[3]
     b0 = lengths_ref[0]
@@ -222,7 +225,7 @@
         ).start()
 
     def project(j):
-        w = weights[pl.ds(j * 16, 16)].reshape(D, 256)
+        w = weights[j].reshape(D, 256)
 
         def rows(b, carry):
             at = pl.ds(b * 3, 3)
@@ -273,16 +276,12 @@
             device_id=mate, device_id_type=MESH,
         ).start()
 
-    def natural(j):
+    def natural(a):
         for g in range(4):
-            part = weights[pl.ds((N_IN + j) * 16 + g * 4, 4)].reshape(384, 256)
-            w_nat[c, j, g * 384 : (g + 1) * 384, :] = jnp.dot(
-                order_ref[...], part, preferred_element_type=F32
+            w_nat[c, a, g * 384 : (g + 1) * 384, :] = jnp.dot(
+                order_ref[...], wout[a, g].reshape(384, 384), preferred_element_type=F32
             ).astype(BF16)
-        pltpu.make_async_remote_copy(
-            src_ref=w_nat.at[c, j], dst_ref=w_nat.at[c, j], send_sem=w_send, recv_sem=w_recv,
-            device_id=mate, device_id_type=MESH,
-        ).start()
+        send(w_nat.at[c, a], w_nat.at[c, a], w_send, w_recv, mate)
 
     def loop(lo, hi, f):
         lax.fori_loop(lo, hi, lambda k, carry: (f(k), carry)[1], 0)
@@ -290,27 +289,44 @@
     gated[0:16, :] = jnp.zeros((16, 128), F32)
     gated[ROWS + 16 : ROWS + 32, :] = jnp.zeros((16, 128), F32)
 
-    loop(0, NCH, z_start)
+    s0(0)
+    s0(1)
     normed_own[8 * (1 - c)] = jnp.zeros((BLK, D), BF16)
     mask_own[8 * (1 - c)] = jnp.zeros((BLK, 128), F32)
-
-    e1(0)
-    loop(0, 2, layer_norm_block)
-    e2(0)
-    loop(2, 4, layer_norm_block)
-    e1(1)
-    e3(0)
-    loop(4, 6, layer_norm_block)
-    e2(1)
-    e4(0)
-    loop(6, 8, layer_norm_block)
-    masks = pl.ds(c, 8)
-    pltpu.make_async_remote_copy(
-        src_ref=mask_own.at[masks], dst_ref=mask_mate.at[masks], send_sem=m_send, recv_sem=m_recv,
-        device_id=mate, device_id_type=MESH,
-    ).start()
     normed_mate[8 * c] = jnp.zeros((BLK, D), BF16)
     mask_mate[8 * c] = jnp.zeros((BLK, 128), F32)
+
+    def norm_step(i):
+        layer_norm_block(i)
+
+        @pl.when(i == 1)
+        def _():
+            s1(0)
+            s0(2)
+
+        @pl.when(i == 2)
+        def _():
+            s1(1)
+            s0(3)
+
+        @pl.when(i == 3)
+        def _():
+            s2(0)
+
+        @pl.when(i == 4)
+        def _():
+            s2(1)
+            s1(2)
+
+        @pl.when(i == 6)
+        def _():
+            s1(3)
+
+    loop(0, 8, norm_step)
+    masks = pl.ds(c, 8)
+    send(mask_own.at[masks], mask_mate.at[masks], m_send, m_recv, mate)
+    s3(0)
+    s2(2)
     wait_for(normed_mate.at[pl.ds(0, 8)], n_send)
     wait_for(mask_mate.at[pl.ds(0, 8)], m_send)
     wait_for(normed_mate.at[pl.ds(0, 8)], n_recv)
@@ -321,31 +337,39 @@
         mask_own[q] = mask_own[q] + mask_mate[q]
 
     loop(0, NB, join)
-
-    def slot(m):
-        pl.when(m < NCH)(lambda: e1(m))
-        pl.when(m < NCH + 1)(lambda: e3(m - 1))
-        e5(m - 2)
-        pl.when(m - 2 < N_IN)(lambda: project(m - 2))
-        pl.when(m - 2 >= N_IN)(lambda: natural(m - 2 - N_IN))
-        pl.when(m < NCH)(lambda: e2(m))
-        pl.when(m < NCH + 1)(lambda: e4(m - 1))
-        pl.when(m - 2 < N_IN)(lambda: convolve(m - 2))
-
-    loop(2, N_IN + 2, slot)
-
-    me_a = x * 4 + y
-    st_a[me_a] = st_own[...]
-
-    def send_a(k):
-        xx, yy = xy_peer(k)
-        pltpu.make_async_remote_copy(
-            src_ref=st_own, dst_ref=st_a.at[me_a], send_sem=sa_send, recv_sem=sa_recv,
-            device_id=device(xx, yy, z, c), device_id_type=MESH,
-        ).start()
-
-    loop(1, 16, send_a)
-    slot(N_IN + 2)
+    s3(1)
+    s2(3)
+    s4(0)
+
+    def compute(j):
+        project(j)
+
+        @pl.when(j == 1)
+        def _():
+            s3(2)
+
+        convolve(j)
+
+        @pl.when(j == 1)
+        def _():
+            s4(1)
+
+        @pl.when(j == 2)
+        def _():
+            s3(3)
+
+        @pl.when(j == 3)
+        def _():
+            s4(2)
+
+    loop(0, N_IN, compute)
+
+    st_a[me_xy] = st_own[...]
+    for k in range(1, 16):
+        send(st_own, st_a.at[me_xy], sa_send, sa_recv, xy_peers[k])
+    s4(3)
+    natural(0)
+    natural(1)
     wait_for(st_a.at[pl.ds(0, 15)], sa_recv)
     all_a = st_a[...]
     mean_a = jnp.sum(all_a[:, 0], axis=0) * (1.0 / 16)
@@ -354,17 +378,8 @@
     st_b0[1] = jnp.sum(all_a[:, 1], axis=0) + PAIR * jnp.sum(off_a * off_a, axis=0)
     me_b = c * 8 + z
     st_b[me_b] = st_b0[...]
-
-    def send_b(k):
-        zz, cc = z_peer(k)
-        pltpu.make_async_remote_copy(
-            src_ref=st_b0, dst_ref=st_b.at[me_b], send_sem=sb_send, recv_sem=sb_recv,
-            device_id=device(x, y, zz, cc), device_id_type=MESH,
-        ).start()
-
-    loop(1, 16, send_b)
-    slot(N_IN + 3)
-    slot(N_IN + 4)
+    for k in range(1, 16):
+        send(st_b0, st_b.at[me_b], sb_send, sb_recv, z_peers[k])
     wait_for(st_b.at[pl.ds(0, 15)], sb_recv)
     for h in range(2):
         part = st_b[h * 8 : h * 8 + 8]
@@ -400,18 +415,24 @@
         chosen = jnp.logical_and(place(i) == r, i < n_own).astype(F32).astype(BF16)
         mine = jnp.dot(chosen, window(act, w), preferred_element_type=F32).astype(BF16)
         rows = pl.ds(t * 8, 8)
-        live = i0 + lax.broadcasted_iota(jnp.int32, (BLK, 256), 0) < n_own
+        live = i0 + lax.broadcasted_iota(jnp.int32, (BLK, 384), 0) < n_own
         for h in range(2):
-            for k in range(N_OUT):
-                lo = h * HALF + k * 256
+            for k in range(2):
+                lo = h * HALF + k * 384
                 branch = jnp.dot(mine, w_nat[h, k], preferred_element_type=F32)
-                res = x_ref[rows, :, lo : lo + 256].reshape(BLK, 256).astype(F32) + branch
-                out_ref[rows, :, lo : lo + 256] = jnp.where(live, res, 0.0).astype(BF16).reshape(8, 16, 256)
+                res = x_ref[rows, :, lo : lo + 384].reshape(BLK, 384).astype(F32) + branch
+                out_ref[rows, :, lo : lo + 384] = jnp.where(live, res, 0.0).astype(BF16).reshape(8, 16, 384)
 
     loop(0, CAP // BLK, finish)
 
     wait_for(zin.at[:, pl.ds(0, 15)], z_send)
-    wait_for(weights.at[pl.ds(0, 135)], ring_send)
+    wait_for(zin_o.at[pl.ds(0, 15)], zo_send)
+    wait_for(weights.at[:, pl.ds(0, 3), 0], r1_send.at[0])
+    wait_for(weights.at[pl.ds(0, 3)], r2_send.at[0])
+    wait_for(weights.at[:, 0], r3_send.at[0])
+    wait_for(wout.at[0, pl.ds(0, 2), pl.ds(0, 3)], r1_send.at[1])
+    wait_for(wout.at[0], r2_send.at[1])
+    wait_for(wout.at[0, pl.ds(0, 2)], r3_send.at[1])
     wait_for(conv.at[pl.ds(0, 6), pl.ds(0, PAIR)], c_send)
     wait_for(w_nat.at[0], w_send)
     wait_for(st_a.at[pl.ds(0, 15)], sa_send)
@@ -429,9 +450,12 @@
         in_specs=[pl.BlockSpec(memory_space=pltpu.SMEM)] + [vmem] * 10,
         out_specs=vmem,
         scratch_shapes=[
-            pltpu.VMEM((2, NCH, 8, 256), BF16),
-            pltpu.VMEM((NCH, 16, 8, 256), BF16),
-            pltpu.VMEM((NCH * 16, 96, 256), BF16),
+            pltpu.VMEM((2, 3, 2, 8, 256), BF16),
+            pltpu.VMEM((2, 2, 8, 384), BF16),
+            pltpu.VMEM((3, 16, 2, 8, 256), BF16),
+            pltpu.VMEM((16, 2, 8, 384), BF16),
+            pltpu.VMEM((N_IN, 4, 4, 96, 256), BF16),
+            pltpu.VMEM((2, 4, 4, 96, 384), BF16),
             pltpu.VMEM((BLK, D), F32),
             pltpu.VMEM((NB, BLK, D), BF16),
             pltpu.VMEM((NB, BLK, D), BF16),
@@ -441,13 +465,13 @@
             pltpu.VMEM((ROWS + 32, 128), F32),
             pltpu.VMEM((12, ROWS, 128), F32),
             pltpu.VMEM((ROWS // 16, 16, D), BF16),
-            pltpu.VMEM((2, N_OUT, D, 256), BF16),
+            pltpu.VMEM((2, 2, D, 384), BF16),
             pltpu.VMEM((2, 6, 1, 128), F32),
             pltpu.VMEM((16, 2, 6, 1, 128), F32),
             pltpu.VMEM((2, 6, 1, 128), F32),
             pltpu.VMEM((16, 2, 6, 1, 128), F32),
             pltpu.VMEM((2, 12, 1, 128), F32),
-            dma, dma((NCH,)), dma, dma((NCH, 3)), dma((NCH, 3)),
+            dma, dma, dma((4,)), dma((2,)), dma((2,)), dma((2,)), dma((4,)), dma((4,)), dma((4,)),
             dma, dma, dma, dma, dma, dma, dma, dma, dma, dma, dma, dma,
         ],
         compiler_params=pltpu.CompilerParams(

time: 133 us -> 98.1 us (0.74)
  Pallas kernels: 124 us -> 89.1 us
    pallas_call x1, Pallas kernels: 124 us -> 89.1 us  [on_device(): pl.pallas_call(kernel, out_shape=jax.ShapeDtypeStruct((CAP // 16, 16, D),...]
where the time goes in v2:
time: 98.1 us; the launch traced here: 97.8 us
  Pallas kernels  89.1 us (91%)
  local copies, waits for them, and re-layouts  8.67 us (9%)
    pallas_call x1, Pallas kernels, on_device(): pl.pallas_call(kernel, out_shape=jax.ShapeDtypeStruct((CAP // 16, 16, D),...  89.1 us
    unnamed x1, local copies, waits for them, and re-layouts  3.49 us

profile of v2, /device:TPU:1, one launch (start us, length us, event | category | flops | bytes accessed | tf_op | source)
XLA Modules:
  0.0 97.8 jit_solution(4920215382805992888)
XLA Ops:
  0.0 1.3 %reshape.23.gain_ref = f32[1,1536]{1,0:T(1,128)} reshape(f32[1536]{0:T(1024)} %param.13) | data formatting | bytes 12288 | tf_op jit(solution)/shard_map/reshape | solution.py:484
  1.3 1.3 %reshape.24.bias_ref = f32[1,1536]{1,0:T(1,128)} reshape(f32[1536]{0:T(1024)} %param.14) | data formatting | bytes 12288 | tf_op jit(solution)/shard_map/reshape | solution.py:484
  2.6 1.3 %reshape.25.bgain_ref = f32[1,1536]{1,0:T(1,128)} reshape(f32[1536]{0:T(1024)} %param.17) | data formatting | bytes 12288 | tf_op jit(solution)/shard_map/reshape | solution.py:485
  3.9 1.3 %reshape.26.bbias_ref = f32[1,1536]{1,0:T(1,128)} reshape(f32[1536]{0:T(1024)} %param.18) | data formatting | bytes 12288 | tf_op jit(solution)/shard_map/reshape | solution.py:485
  5.2 89.1 %shard_map.109 = bf16[56,16,1536]{2,1,0:T(8,128)(2,1)} custom-call(s32[4]{0:T(128)} %bitcast.5, bf16[56,16,1536]{2,1,0:T(8,128)(2,1)} %bitcast.4, f32[1,1536]{1,0:T(1,128)} %reshape.23.gain_ref, f32[1,1536]{1,0:T(1,128)} %reshape.24.bias_ref, bf16[6,3072]{1,0:T(8,128)(2,1)} %w_in_ref.1, bf16[6,1536]{1,0:T(8,128)(2,1)} %w_out_ref.1, f32[31,1536]{1,0:T(8,128)} %taps_ref.1, ...), custom_call_target="tpu_custom_call" | custom-call | flops 20000000000 | bytes 10000000 | tf_op jit(solution)/shard_map/pallas_call | solution.py:447
  94.3 3.5 %copy.13 = bf16[1,896,1536]{2,1,0:T(8,128)(2,1)} copy(bf16[1,896,1536]{2,1,0:T(8,128)(2,1)} %bitcast.3) | data formatting | bytes 5505024

commit v3 on v2

--- a/solution.py
+++ b/solution.py
@@ -47,12 +47,13 @@
 
 
 def kernel(
-    lengths_ref, x_ref, gain_ref, bias_ref, w_in_ref, w_out_ref, taps_ref, bgain_ref, bbias_ref,
+    lengths_ref, x_ref, gain_1d, bias_1d, w_in_ref, w_out_ref, taps_ref, bgain_1d, bbias_1d,
     order_ref, pick_ref,
     out_ref,
-    slab, slab_o, zin, zin_o, weights, wout, xs, normed_own, normed_mate, mask_own, mask_mate,
-    proj, gated, conv, act, w_nat, st_own, st_a, st_b0, st_b, stats,
-    z_send, zo_send, z_recv, r1_send, r2_send, r3_send, r1_recv, r2_recv, r3_recv, n_send, n_recv, m_send, m_recv,
+    gain_ref, bias_ref, bgain_ref, bbias_ref, slab, slab_o, zin, both_o, zin_o, weights, wout, xs, normed_own, normed_mate, mask_own, mask_mate,
+    proj, gated, conv, act, st_own, st_a, st_b0, st_b, stats,
+    bo_send, bo_recv, z_send, zo_send, z_recv, zo_recv, r1_send, r2_send, r3_send, r1_recv, r2_recv, r3_recv,
+    o_send, o_recv, n_send, n_recv, m_send, m_recv,
     c_send, c_recv, w_send, w_recv, sa_send, sa_recv, sb_send, sb_recv,
 ):
     dp = lax.axis_index("dp")
@@ -72,6 +73,7 @@
     mate = (flip(dp, flips, 1), y)
     z_peers = [(flip(dp, flips, k), y) for k in range(16)]
     xy_peers = [(flip(dp, flips, (k >> 2) << 4), flip(y, y_flips, k & 3)) for k in range(16)]
+    zs_at = [lax.rem(z + k, 8) for k in range(8)]
     xs_at = [lax.rem(x + k, 4) for k in range(4)]
     ys_at = [lax.rem(y + k, 4) for k in range(4)]
     me_z = z * 2 + c
@@ -81,6 +83,11 @@
     for k in range(1, 16):
         pl.semaphore_signal(barrier, 1, device_id=z_peers[k], device_id_type=MESH)
         pl.semaphore_signal(barrier, 1, device_id=xy_peers[k], device_id_type=MESH)
+
+    for vector, ref in (
+        (gain_1d, gain_ref), (bias_1d, bias_ref), (bgain_1d, bgain_ref), (bbias_1d, bbias_ref)
+    ):
+        ref[...] = vector[...].reshape(1, D)
 
     slab[...] = jnp.zeros_like(slab)
     slab_o[...] = jnp.zeros_like(slab_o)
@@ -93,8 +100,8 @@
             lo = h * HALF + j * 384
             slab_o[h, j, 0:6, :] = w_out_ref[:, lo : lo + 384]
     for p in range(3):
-        zin[p, me_z] = slab[c, p]
-    zin_o[me_z] = slab_o[c]
+        zin[me_z, p] = slab[c, p]
+    both_o[c] = slab_o[c]
 
     pl.semaphore_wait(barrier, 30)
 
@@ -110,28 +117,21 @@
     def s0(p):
         for k in range(1, 16):
             other = 1 - c if k % 2 else c
-            if p < 3:
-                send(slab.at[other, p], zin.at[p, me_z], z_send, z_recv.at[p], z_peers[k])
-            else:
-                send(slab_o.at[other], zin_o.at[me_z], zo_send, z_recv.at[p], z_peers[k])
+            part = pl.ds(p, 1 + p)
+            send(slab.at[other, part], zin.at[me_z, part], z_send, z_recv.at[p], z_peers[k])
 
     def chunk(p, a):
-        return weights.at[2 * p + a] if p < 3 else wout.at[a]
-
-    def kind(p):
-        return 0 if p < 3 else 1
+        return weights.at[2 * p + a]
 
     def for_core(f):
         pl.when(c == 0)(lambda: f(0))
         pl.when(c == 1)(lambda: f(1))
 
     def s1(p):
-        if p < 3:
-            wait_for(zin.at[0, pl.ds(0, 15)], z_recv.at[p])
-        else:
-            wait_for(zin_o.at[pl.ds(0, 15)], z_recv.at[p])
+        if p < 2:
+            wait_for(zin.at[pl.ds(0, 15), pl.ds(0, 1 + p)], z_recv.at[p])
         for a in range(2):
-            rows = (zin[p, :, a] if p < 3 else zin_o[:, a]).reshape(128, 256 if p < 3 else 384)
+            rows = zin[:, p, a].reshape(128, 256)
             chunk(p, a)[x, y] = jnp.dot(
                 pick_ref[...], rows, preferred_element_type=F32
             ).astype(BF16)
@@ -141,7 +141,7 @@
                 ref = chunk(p, a).at[x, y]
                 for k in (1, 3, 2):
                     to = (dp + (xs_at[k] - x) * 16, y) if (v + a) % 2 == 0 else (dp, ys_at[k])
-                    send(ref, ref, r1_send.at[kind(p)], r1_recv.at[p], to)
+                    send(ref, ref, r1_send, r1_recv.at[p], to)
 
         for_core(go)
 
@@ -160,7 +160,7 @@
             for a in range(2):
                 ref = second(p, a, v, 0, pl.ds(0, 4))
                 for k in (1, 3):
-                    send(ref, ref, r2_send.at[kind(p)], r2_recv.at[p], second_to(a, v, k))
+                    send(ref, ref, r2_send, r2_recv.at[p], second_to(a, v, k))
 
         for_core(go)
 
@@ -171,12 +171,55 @@
             for a in range(2):
                 for k, part in ((1, pl.ds(0, 2)), (3, pl.ds(2, 2))):
                     ref = second(p, a, v, 4 - k, part)
-                    send(ref, ref, r3_send.at[kind(p)], r3_recv.at[p], second_to(a, v, k))
+                    send(ref, ref, r3_send, r3_recv.at[p], second_to(a, v, k))
 
         for_core(go)
 
     def s4(p):
         wait_for(chunk(p, 0).at[pl.ds(0, 2)], r3_recv.at[p])
+
+    def o0():
+        wait_for(both_o.at[0], bo_recv)
+        zin_o[x, :, y] = both_o[...]
+        for k in range(1, 16):
+            send(both_o, zin_o.at[x, :, y], zo_send, zo_recv, xy_peers[k])
+
+    def bundle(a, k, part=pl.ds(0, 4)):
+        return wout.at[c, a, part, zs_at[k]]
+
+    def around(a, t, k, to, part=pl.ds(0, 4)):
+        ref = bundle(a, k, part)
+        send(ref, ref, o_send.at[0 if t < 3 else 1], o_recv.at[a, t], (dp + (zs_at[to] - z) * 2, y))
+
+    def to_mate(a, k):
+        send(bundle(a, k), bundle(a, k), w_send, w_recv, mate)
+
+    def o1():
+        wait_for(zin.at[pl.ds(0, 15)], zo_recv)
+        for a in range(2):
+            for g in range(2):
+                rows = zin_o[2 * g : 2 * g + 2, :, :, a].reshape(128, 384)
+                block = jnp.dot(pick_ref[...], rows, preferred_element_type=F32).astype(BF16)
+                wout[c, a, 2 * g, z] = block[:48]
+                wout[c, a, 2 * g + 1, z] = block[48:]
+            around(a, 0, 0, 1)
+            around(a, 0, 0, 7)
+            to_mate(a, 0)
+
+    def o2(t, a):
+        wait_for(wout.at[0, a, :, pl.ds(0, 2)], o_recv.at[a, t - 1])
+        if t < 3:
+            around(a, t, 8 - t, 1)
+            around(a, t, t, 7)
+        else:
+            around(a, t, 5, 1, pl.ds(0, 2))
+            around(a, t, 3, 7, pl.ds(2, 2))
+        to_mate(a, t)
+        to_mate(a, 8 - t)
+
+    def o3(a):
+        wait_for(wout.at[0, a, :, 0], o_recv.at[a, 3])
+        to_mate(a, 4)
 
     n_own = lengths_ref[0] + lengths_ref[1] + lengths_ref[2] + lengths_ref[3]
     b0 = lengths_ref[0]
@@ -213,12 +256,7 @@
             normed_own[q, at, :] = jnp.where(m > 0.0, res, 0.0).astype(BF16)
             return carry
 
-        lax.fori_loop(0, BLK // 16, rows, 0)
-        for g in range(4):
-            cols = slice(g * 384, (g + 1) * 384)
-            normed_own[q, :, cols] = jnp.dot(
-                normed_own[q, :, cols], order_ref[...], preferred_element_type=F32
-            ).astype(BF16)
+        lax.fori_loop(0, BLK // 16, rows, 0, unroll=4)
         pltpu.make_async_remote_copy(
             src_ref=normed_own.at[q], dst_ref=normed_mate.at[q], send_sem=n_send, recv_sem=n_recv,
             device_id=mate, device_id_type=MESH,
@@ -276,19 +314,13 @@
             device_id=mate, device_id_type=MESH,
         ).start()
 
-    def natural(a):
-        for g in range(4):
-            w_nat[c, a, g * 384 : (g + 1) * 384, :] = jnp.dot(
-                order_ref[...], wout[a, g].reshape(384, 384), preferred_element_type=F32
-            ).astype(BF16)
-        send(w_nat.at[c, a], w_nat.at[c, a], w_send, w_recv, mate)
-
     def loop(lo, hi, f):
         lax.fori_loop(lo, hi, lambda k, carry: (f(k), carry)[1], 0)
 
     gated[0:16, :] = jnp.zeros((16, 128), F32)
     gated[ROWS + 16 : ROWS + 32, :] = jnp.zeros((16, 128), F32)
 
+    send(slab_o.at[1 - c], both_o.at[c], bo_send, bo_recv, mate)
     s0(0)
     s0(1)
     normed_own[8 * (1 - c)] = jnp.zeros((BLK, D), BF16)
@@ -299,77 +331,73 @@
     def norm_step(i):
         layer_norm_block(i)
 
-        @pl.when(i == 1)
-        def _():
-            s1(0)
-            s0(2)
-
-        @pl.when(i == 2)
-        def _():
-            s1(1)
-            s0(3)
-
-        @pl.when(i == 3)
-        def _():
-            s2(0)
-
-        @pl.when(i == 4)
-        def _():
-            s2(1)
-            s1(2)
-
-        @pl.when(i == 6)
-        def _():
-            s1(3)
+        for at, steps in (
+            (0, (o0,)),
+            (2, (lambda: s1(0),)),
+            (6, (lambda: s2(0), lambda: s1(1))),
+        ):
+            @pl.when(i == at)
+            def _(steps=steps):
+                for step in steps:
+                    step()
 
     loop(0, 8, norm_step)
     masks = pl.ds(c, 8)
     send(mask_own.at[masks], mask_mate.at[masks], m_send, m_recv, mate)
-    s3(0)
-    s2(2)
     wait_for(normed_mate.at[pl.ds(0, 8)], n_send)
     wait_for(mask_mate.at[pl.ds(0, 8)], m_send)
     wait_for(normed_mate.at[pl.ds(0, 8)], n_recv)
     wait_for(mask_mate.at[pl.ds(0, 8)], m_recv)
 
-    def join(q):
-        normed_own[q] = normed_own[q] + normed_mate[q]
-        mask_own[q] = mask_own[q] + mask_mate[q]
-
-    loop(0, NB, join)
-    s3(1)
-    s2(3)
+    def join(b):
+        at = pl.ds(b * 3, 3)
+        both = (normed_own[at] + normed_mate[at]).reshape(3 * BLK, D)
+        for g in range(4):
+            cols = slice(g * 384, (g + 1) * 384)
+            normed_own[at, :, cols] = jnp.dot(
+                both[:, cols], order_ref[...], preferred_element_type=F32
+            ).astype(BF16).reshape(3, BLK, 384)
+        mask_own[at] = mask_own[at] + mask_mate[at]
+
+    def join_step(b):
+        join(b)
+
+        @pl.when(b == 0)
+        def _():
+            o1()
+
+    loop(0, NB // 3, join_step)
+    s3(0)
+    s2(1)
+    s1(2)
+    o2(1, 0)
     s4(0)
 
     def compute(j):
         project(j)
-
-        @pl.when(j == 1)
-        def _():
-            s3(2)
-
+        for at, steps in (
+            (0, (lambda: o2(1, 1),)), (1, (lambda: o2(2, 1),)),
+            (2, (lambda: s3(2),)), (3, (lambda: o2(3, 1),)), (5, (lambda: o3(1),)),
+        ):
+            @pl.when(j == at)
+            def _(steps=steps):
+                for step in steps:
+                    step()
         convolve(j)
-
-        @pl.when(j == 1)
-        def _():
-            s4(1)
-
-        @pl.when(j == 2)
-        def _():
-            s3(3)
-
-        @pl.when(j == 3)
-        def _():
-            s4(2)
+        for at, steps in (
+            (0, (lambda: s3(1), lambda: s2(2), lambda: o2(2, 0))), (1, (lambda: s4(1),)),
+            (2, (lambda: o2(3, 0),)), (3, (lambda: s4(2),)), (4, (lambda: o3(0),)),
+        ):
+            @pl.when(j == at)
+            def _(steps=steps):
+                for step in steps:
+                    step()
 
     loop(0, N_IN, compute)
 
     st_a[me_xy] = st_own[...]
     for k in range(1, 16):
         send(st_own, st_a.at[me_xy], sa_send, sa_recv, xy_peers[k])
-    s4(3)
-    natural(0)
-    natural(1)
     wait_for(st_a.at[pl.ds(0, 15)], sa_recv)
     all_a = st_a[...]
     mean_a = jnp.sum(all_a[:, 0], axis=0) * (1.0 / 16)
@@ -393,7 +421,7 @@
 
     at_mine = pl.ds(pl.multiple_of(c * BLK, BLK), PAIR)
     wait_for(conv.at[pl.ds(0, 6), pl.ds(0, PAIR)], c_recv)
-    wait_for(w_nat.at[0], w_recv)
+    wait_for(wout.at[0], w_recv)
 
     def activate(qi):
         q = qi + c
@@ -419,22 +447,24 @@
         for h in range(2):
             for k in range(2):
                 lo = h * HALF + k * 384
-                branch = jnp.dot(mine, w_nat[h, k], preferred_element_type=F32)
+                branch = jnp.dot(
+                    mine, wout[h, k].reshape(D, 384), preferred_element_type=F32
+                )
                 res = x_ref[rows, :, lo : lo + 384].reshape(BLK, 384).astype(F32) + branch
                 out_ref[rows, :, lo : lo + 384] = jnp.where(live, res, 0.0).astype(BF16).reshape(8, 16, 384)
 
     loop(0, CAP // BLK, finish)
 
-    wait_for(zin.at[:, pl.ds(0, 15)], z_send)
-    wait_for(zin_o.at[pl.ds(0, 15)], zo_send)
-    wait_for(weights.at[:, pl.ds(0, 3), 0], r1_send.at[0])
-    wait_for(weights.at[pl.ds(0, 3)], r2_send.at[0])
-    wait_for(weights.at[:, 0], r3_send.at[0])
-    wait_for(wout.at[0, pl.ds(0, 2), pl.ds(0, 3)], r1_send.at[1])
-    wait_for(wout.at[0], r2_send.at[1])
-    wait_for(wout.at[0, pl.ds(0, 2)], r3_send.at[1])
+    wait_for(zin.at[pl.ds(0, 15)], z_send)
+    wait_for(both_o.at[0], bo_send)
+    wait_for(zin.at[pl.ds(0, 15)], zo_send)
+    wait_for(weights.at[:, pl.ds(0, 3), 0], r1_send)
+    wait_for(weights.at[pl.ds(0, 3)], r2_send)
+    wait_for(weights.at[:, 0], r3_send)
+    wait_for(wout.at[0, :, :, pl.ds(0, 6)], o_send.at[0])
+    wait_for(wout.at[0, :, :, 0], o_send.at[1])
     wait_for(conv.at[pl.ds(0, 6), pl.ds(0, PAIR)], c_send)
-    wait_for(w_nat.at[0], w_send)
+    wait_for(wout.at[0], w_send)
     wait_for(st_a.at[pl.ds(0, 15)], sa_send)
     wait_for(st_b.at[pl.ds(0, 15)], sb_send)
 
@@ -450,12 +480,15 @@
         in_specs=[pl.BlockSpec(memory_space=pltpu.SMEM)] + [vmem] * 10,
         out_specs=vmem,
         scratch_shapes=[
+            pltpu.VMEM((1, D), F32), pltpu.VMEM((1, D), F32),
+            pltpu.VMEM((1, D), F32), pltpu.VMEM((1, D), F32),
             pltpu.VMEM((2, 3, 2, 8, 256), BF16),
             pltpu.VMEM((2, 2, 8, 384), BF16),
-            pltpu.VMEM((3, 16, 2, 8, 256), BF16),
-            pltpu.VMEM((16, 2, 8, 384), BF16),
+            pltpu.VMEM((16, 3, 2, 8, 256), BF16),
+            pltpu.VMEM((2, 2, 8, 384), BF16),
+            pltpu.VMEM((4, 2, 4, 2, 8, 384), BF16),
             pltpu.VMEM((N_IN, 4, 4, 96, 256), BF16),
-            pltpu.VMEM((2, 4, 4, 96, 384), BF16),
+            pltpu.VMEM((2, 2, 4, 8, 48, 384), BF16),
             pltpu.VMEM((BLK, D), F32),
             pltpu.VMEM((NB, BLK, D), BF16),
             pltpu.VMEM((NB, BLK, D), BF16),
@@ -465,13 +498,13 @@
             pltpu.VMEM((ROWS + 32, 128), F32),
             pltpu.VMEM((12, ROWS, 128), F32),
             pltpu.VMEM((ROWS // 16, 16, D), BF16),
-            pltpu.VMEM((2, 2, D, 384), BF16),
             pltpu.VMEM((2, 6, 1, 128), F32),
             pltpu.VMEM((16, 2, 6, 1, 128), F32),
             pltpu.VMEM((2, 6, 1, 128), F32),
             pltpu.VMEM((16, 2, 6, 1, 128), F32),
             pltpu.VMEM((2, 12, 1, 128), F32),
-            dma, dma, dma((4,)), dma((2,)), dma((2,)), dma((2,)), dma((4,)), dma((4,)), dma((4,)),
+            dma, dma, dma, dma, dma((3,)), dma, dma, dma, dma, dma((3,)), dma((3,)), dma((3,)),
+            dma((2,)), dma((2, 4)),
             dma, dma, dma, dma, dma, dma, dma, dma, dma, dma, dma, dma,
         ],
         compiler_params=pltpu.CompilerParams(
@@ -481,8 +514,8 @@
             flops=20 * 10**9, bytes_accessed=10**7, transcendentals=4 * 10**6
         ),
     )(
-        lengths.reshape(4), frames_in.reshape(CAP // 16, 16, D), norm_gain.reshape(1, D), norm_bias.reshape(1, D),
-        w_in, w_out, taps, batch_gain.reshape(1, D), batch_bias.reshape(1, D),
+        lengths.reshape(4), frames_in.reshape(CAP // 16, 16, D), norm_gain, norm_bias,
+        w_in, w_out, taps, batch_gain, batch_bias,
         jnp.asarray(feature_order(), BF16), jnp.asarray(compaction(), BF16),
     )
     return out.reshape(1, CAP, D)

time: 98.1 us -> 89.1 us (0.908)
  local copies, waits for them, and re-layouts: 8.67 us -> 3.49 us
  Pallas kernels: 89.1 us -> 85.5 us
    reshape x4 -> x0, local copies, waits for them, and re-layouts: 5.18 us -> none  [the longest x1 1.3 us: on_device(): batch_bias.reshape(1, D)]
    pallas_call x1, Pallas kernels: 89.1 us -> 85.5 us  [on_device(): pl.pallas_call(kernel, out_shape=jax.ShapeDtypeStruct((CAP // 16, 16, D),...]
where the time goes in v3:
time: 89.1 us; the launch traced here: 89 us
  Pallas kernels  85.5 us (96%)
  local copies, waits for them, and re-layouts  3.49 us (4%)
    pallas_call x1, Pallas kernels, on_device(): pl.pallas_call(kernel, out_shape=jax.ShapeDtypeStruct((CAP // 16, 16, D),...  85.5 us
    unnamed x1, local copies, waits for them, and re-layouts  3.49 us

profile of v3, /device:TPU:1, one launch (start us, length us, event | category | flops | bytes accessed | tf_op | source)
XLA Modules:
  0.0 89.0 jit_solution(4677316483154202864)
XLA Ops:
  0.0 85.5 %shard_map.109 = bf16[56,16,1536]{2,1,0:T(8,128)(2,1)} custom-call(s32[4]{0:T(128)} %bitcast.5, bf16[56,16,1536]{2,1,0:T(8,128)(2,1)} %bitcast.4, f32[1536]{0:T(1024)} %gain_1d.1, f32[1536]{0:T(1024)} %bias_1d.1, bf16[6,3072]{1,0:T(8,128)(2,1)} %w_in_ref.1, bf16[6,1536]{1,0:T(8,128)(2,1)} %w_out_ref.1, f32[31,1536]{1,0:T(8,128)} %taps_ref.1, f32[1536]{0:T(1024)} %bgain_1d.1, ...), custom_call_target="tpu_custom_call" | custom-call | flops 20000000000 | bytes 10000000 | tf_op jit(solution)/shard_map/pallas_call | solution.py:477
  85.5 3.5 %copy.13 = bf16[1,896,1536]{2,1,0:T(8,128)(2,1)} copy(bf16[1,896,1536]{2,1,0:T(8,128)(2,1)} %bitcast.3) | data formatting | bytes 5505024

commit v4 on v3

--- a/solution.py
+++ b/solution.py
@@ -266,17 +266,17 @@
         w = weights[j].reshape(D, 256)
 
         def rows(b, carry):
-            at = pl.ds(b * 3, 3)
+            at = pl.ds(0, 9)
             proj[...] = jnp.dot(
-                normed_own[at].reshape(3 * BLK, D), w, preferred_element_type=F32
+                normed_own[at].reshape(9 * BLK, D), w, preferred_element_type=F32
             )
             v = proj[:, 0:128]
             g = proj[:, 128:256]
             res = v * jax.nn.sigmoid(g)
-            gated[pl.ds(pl.multiple_of(16 + b * 3 * BLK, 16), 3 * BLK), :] = res.astype(BF16).astype(F32)
+            gated[pl.ds(16, 9 * BLK), :] = res.astype(BF16).astype(F32)
             return carry
 
-        lax.fori_loop(0, NB // 3, rows, 0)
+        rows(0, 0)
 
     def convolve(j):
         cc = c * N_IN + j
@@ -494,7 +494,7 @@
             pltpu.VMEM((NB, BLK, D), BF16),
             pltpu.VMEM((NB, BLK, 128), F32),
             pltpu.VMEM((NB, BLK, 128), F32),
-            pltpu.VMEM((3 * BLK, 256), F32),
+            pltpu.VMEM((9 * BLK, 256), F32),
             pltpu.VMEM((ROWS + 32, 128), F32),
             pltpu.VMEM((12, ROWS, 128), F32),
             pltpu.VMEM((ROWS // 16, 16, D), BF16),

time: 89.1 us -> 88 us (0.988)
  Pallas kernels: 85.5 us -> 84.4 us
    pallas_call x1, Pallas kernels: 85.5 us -> 84.4 us  [on_device(): pl.pallas_call(kernel, out_shape=jax.ShapeDtypeStruct((CAP // 16, 16, D),...]
where the time goes in v4:
time: 88 us; the launch traced here: 87.9 us
  Pallas kernels  84.4 us (96%)
  local copies, waits for them, and re-layouts  3.49 us (4%)
    pallas_call x1, Pallas kernels, on_device(): pl.pallas_call(kernel, out_shape=jax.ShapeDtypeStruct((CAP // 16, 16, D),...  84.4 us
    unnamed x1, local copies, waits for them, and re-layouts  3.49 us

profile of v4, /device:TPU:1, one launch (start us, length us, event | category | flops | bytes accessed | tf_op | source)
XLA Modules:
  0.0 87.9 jit_solution(9716956721809130648)
XLA Ops:
  0.0 84.4 %shard_map.109 = bf16[56,16,1536]{2,1,0:T(8,128)(2,1)} custom-call(s32[4]{0:T(128)} %bitcast.5, bf16[56,16,1536]{2,1,0:T(8,128)(2,1)} %bitcast.4, f32[1536]{0:T(1024)} %gain_1d.1, f32[1536]{0:T(1024)} %bias_1d.1, bf16[6,3072]{1,0:T(8,128)(2,1)} %w_in_ref.1, bf16[6,1536]{1,0:T(8,128)(2,1)} %w_out_ref.1, f32[31,1536]{1,0:T(8,128)} %taps_ref.1, f32[1536]{0:T(1024)} %bgain_1d.1, ...), custom_call_target="tpu_custom_call" | custom-call | flops 20000000000 | bytes 10000000 | tf_op jit(solution)/shard_map/pallas_call | solution.py:477
  84.4 3.5 %copy.13 = bf16[1,896,1536]{2,1,0:T(8,128)(2,1)} copy(bf16[1,896,1536]{2,1,0:T(8,128)(2,1)} %bitcast.3) | data formatting | bytes 5505024
